TPU v7x, 128 devices: a whole 4x4x4 slice. The times are simulated.
128 devices in a mesh: aux: 4 (over x), pair: 32 (over z, y, core).
Axes of the slice: x: 4, y: 4, z: 4, core: 2. Of those that a mesh axis runs over, the one named last changes fastest.
Arguments:
- orbital_slabs: bfloat16 [128, 1024, 768], P('pair', 'aux'), may hold values from -2.5 to 2.5
- pno_maps: bfloat16 [512, 768, 256], P('pair'), may hold values from -0.21875 to 0.21875
- intersections: bfloat16 [512, 8, 256, 256], P('pair', 'aux'), may hold values from -0.375 to 0.375
- pno_energy: float32 [512, 256], P('pair'), may hold values from 0.25 to 2
- occ_energy: float32 [128], replicated, may hold values from -1 to -0.25
- pair_orbitals: int32 [512, 2], replicated, may hold values from 0 to 127, as said below
- partners: int32 [512, 8], replicated, may hold values from 0 to 511, as said below
- live: int32 [512], P('pair'), may hold values from 0 to 1, as said below
Outputs:
- amplitudes: bfloat16 [512, 256, 256], P('pair')
- pair_energy: float32 [512], P('pair')
Inputs may be any that keep to these rules, and one draw needn't show every extreme that they name: `pair_orbitals`: each pair names two different orbitals. The pairs of one cluster of 16 slots (padding slots too) name at most one orbital of each block of 4 consecutive orbitals. `partners`: every partner is a live pair. All 128 partner entries of one cluster of 16 slots together name at most one pair of each cluster. In each cluster of 16 slots the live pairs come first and there is at least one; some cluster is full.
All inputs are finite; a program needn't handle non-finite values.
Results may differ from a plain program's by a relative error of at most 0.0066.
Values may be sent and summed in bfloat16 or wider, within the bound.
No kernel may reach another device: no remote copies, remote signals or barrier semaphores. Data moves between devices by JAX's collectives and lax.ppermute only.
A program may use at most 128 MiB of HBM per device.

v0:
```python
import jax
import jax.numpy as jnp
from jax import lax
from jax.sharding import PartitionSpec as P

ITERS = 2
damping = 0.7


def on_device(
    orbital_slabs, pno_maps, intersections, pno_energy, occ_energy, pair_orbitals, partners, live
):
    clusters = lax.axis_size("pair")
    cluster = lax.axis_index("pair")
    aux_row = lax.axis_index("aux")
    orb_count = orbital_slabs.shape[0]
    pair_count = pno_maps.shape[0]
    columns = intersections.shape[1]
    width = intersections.shape[-1]
    wanted = pair_orbitals.reshape(clusters, 2 * pair_count)
    owned = cluster * orb_count + jnp.arange(orb_count, dtype=jnp.int32)
    needed = jnp.any(wanted[:, :, None] == owned[None, None, :], axis=1).astype(jnp.bfloat16)
    outgoing = jnp.dot(
        needed, orbital_slabs.reshape(orb_count, -1), preferred_element_type=jnp.float32
    )
    outgoing = outgoing.astype(jnp.bfloat16).reshape((clusters,) + orbital_slabs.shape[1:])
    my_orbitals = lax.dynamic_slice_in_dim(pair_orbitals, cluster * pair_count, pair_count, 0)
    owner_index = my_orbitals // orb_count
    incoming = lax.all_to_all(outgoing, "pair", split_axis=0, concat_axis=0, tiled=True)
    left = jnp.take(incoming, owner_index[:, 0], axis=0)
    right = jnp.take(incoming, owner_index[:, 1], axis=0)
    left_pno = jnp.einsum(
        "pav,pvn->pan", left, pno_maps, preferred_element_type=jnp.float32
    ).astype(jnp.bfloat16)
    right_pno = jnp.einsum(
        "pav,pvn->pan", right, pno_maps, preferred_element_type=jnp.float32
    ).astype(jnp.bfloat16)
    left_pno, right_pno = (left_pno, right_pno)
    partial_coulomb = jnp.einsum(
        "pan,pam->pnm", left_pno, right_pno, preferred_element_type=jnp.float32
    )
    occupied = jnp.sum(jnp.take(occ_energy, my_orbitals), axis=1)
    denominator = pno_energy[:, :, None] + pno_energy[:, None, :] - occupied[:, None, None]
    weights = live.astype(jnp.float32)
    all_refs = partners.reshape(clusters, pair_count, -1)
    coulomb = lax.psum(partial_coulomb, "aux")
    row_refs = lax.dynamic_slice_in_dim(all_refs, aux_row * columns, columns, 2).reshape(
        clusters, pair_count * columns
    )
    weights = weights[:, None, None]
    amplitude = -weights * coulomb / denominator
    coulomb_half = coulomb.astype(jnp.bfloat16)
    my_pairs = cluster * pair_count + jnp.arange(pair_count, dtype=jnp.int32)
    sending = jnp.any(row_refs[:, :, None] == my_pairs[None, None, :], axis=1).astype(jnp.bfloat16)
    my_refs = lax.dynamic_slice_in_dim(row_refs, cluster, 1, 0).reshape(-1)
    ref_sources = my_refs // pair_count
    ref_rows = intersections.shape[0]
    ref_cols = intersections.shape[1]
    flat_intersections = intersections.reshape(ref_rows * ref_cols, width, width)
    for sweep in range(ITERS):
        local_half = amplitude.astype(jnp.bfloat16)
        outgoing_amps = jnp.dot(
            sending, local_half.reshape(pair_count, -1), preferred_element_type=jnp.float32
        )
        outgoing_amps = outgoing_amps.astype(jnp.bfloat16).reshape(clusters, width, width)
        fetched = jnp.take(
            lax.all_to_all(outgoing_amps, "pair", split_axis=0, concat_axis=0, tiled=True),
            ref_sources,
            axis=0,
        )
        rotated = jnp.einsum(
            "kab,kbc->kac", flat_intersections, fetched, preferred_element_type=jnp.float32
        )
        rotated = rotated.astype(jnp.bfloat16)
        rotated = rotated.reshape(ref_rows, ref_cols, width, width)
        coupling_terms = jnp.einsum(
            "prac,prdc->pad", rotated, intersections, preferred_element_type=jnp.float32
        )
        coupled = lax.psum(coupling_terms, "aux")
        product = jnp.einsum(
            "pab,pcb->pac", local_half, coulomb_half, preferred_element_type=jnp.float32
        ).astype(jnp.bfloat16)
        quadratic = (
            jnp.einsum("pac,pcd->pad", product, local_half, preferred_element_type=jnp.float32)
            / width
        )
        residual = coulomb + denominator * amplitude - coupled + quadratic
        amplitude = weights * (amplitude - damping * residual / denominator)
    result = amplitude.astype(jnp.bfloat16)
    energy = weights[:, 0, 0] * jnp.sum(coulomb * amplitude, axis=(1, 2))
    return (result, energy)


def solution(mesh):
    placed = (
        P("pair", "aux", None),
        P("pair", None, None),
        P("pair", "aux", None, None),
        P("pair", None),
        P(),
        P(),
        P(),
        P("pair"),
    )
    return jax.shard_map(
        on_device,
        mesh=mesh,
        in_specs=placed,
        out_specs=(P("pair", None, None), P("pair")),
        check_vma=False,
    )
```

profile of v0, /device:TPU:1, one launch (start us, length us, event | category | flops | bytes accessed | tf_op | source)
XLA Modules:
  0.0 679.0 jit_solution(8952732491503904884)
XLA Ops:
  7.2 0.8 copy.31
  8.0 0.1 eq.30
  8.2 2.6 copy.47
  10.8 0.2 compare_reduce_fusion.1
  11.0 3.7 convolution_convert_fusion
  14.8 6.4 copy.48
  21.2 9.6 %all-to-all-start = ((bf16[32,256,768]{2,1,0:T(8,128)(2,1)}), bf16[32,256,768]{2,1,0:T(8,128)(2,1)}, u32[]{:S(2)}, u32[]{:S(2)}) async-start(bf16[32,256,768]{2,1,0:T(8,128)(2,1)} %bitcast.43), calls=%async_computation | async-start | bytes 25165824 | tf_op jit(solution)/shard_map/all_to_all | solution.py:29
  30.9 0.2 all-reduce.4.cloned.1.call-start
  31.1 0.2 slice_reduce_fusion.1
  31.4 151.6 %all-to-all-done = bf16[32,256,768]{2,1,0:T(8,128)(2,1)} async-done(((bf16[32,256,768]{2,1,0:T(8,128)(2,1)}), bf16[32,256,768]{2,1,0:T(8,128)(2,1)}, u32[]{:S(2)}, u32[]{:S(2)}) %all-to-all-start) | async-done | bytes 12582944 | tf_op jit(solution)/shard_map/all_to_all | solution.py:29
  183.0 8.1 %gather_fusion.2 = bf16[16,256,768]{2,1,0:T(8,128)(2,1)} fusion(bf16[32,256,768]{2,1,0:T(8,128)(2,1)} %all-to-all-done, s32[1024]{0:T(1024)S(1)} %pad_clamp_fusion.2), kind=kCustom, calls=%fused_computation.2.clone | custom fusion | bytes 12582976 | tf_op jit(solution)/shard_map/jit(_take)/gather | solution.py:31
  191.1 6.4 fusion
  197.6 8.1 %gather_fusion.1 = bf16[16,256,768]{2,1,0:T(8,128)(2,1)} fusion(bf16[32,256,768]{2,1,0:T(8,128)(2,1)} %all-to-all-done, s32[1024]{0:T(1024)S(1)} %pad_clamp_fusion.3), kind=kCustom, calls=%fused_computation.clone | custom fusion | bytes 12582976 | tf_op jit(solution)/shard_map/jit(_take)/gather | solution.py:30
  205.7 9.0 %fusion.26 = f32[16,256,256]{2,1,0:T(8,128)} fusion(bf16[16,256,256]{2,1,0:T(8,128)(2,1)S(1)} %fusion, bf16[16,768,256]{2,1,0:T(8,128)(2,1)} %param.13, bf16[16,256,768]{2,1,0:T(8,128)(2,1)} %gather_fusion.1, pred[16]{0:T(512)(128)(4,1)S(1)} %get-tuple-element.18), kind=kOutput, calls=%fused_computation.36 | convolution fusion | flops 2151677952 | bytes 18874384 | tf_op jit(solution)/shard_map/pan,pam->pnm/dot_general | solution.py:39
  214.8 0.0 all-reduce.4.cloned.1.call-update
  214.8 0.1 reshape.114
  214.9 0.7 gather_fusion
  215.6 0.1 reshape.113
  215.7 0.1 reshape.71
  215.9 0.1 copy.34
  215.9 0.1 copy.35
  216.0 0.1 select_reduce_fusion
  216.1 0.7 compare_reduce_fusion
  216.9 95.4 %all-reduce.4.cloned.1.call-done = f32[16,256,256]{2,1,0:T(8,128)} async-done(((f32[16,256,256]{2,1,0:T(8,128)}), f32[16,256,256]{2,1,0:T(8,128)}) %all-reduce.4.cloned.1.call-update) | async-done | bytes 4194320 | tf_op jit(solution)/shard_map/psum | solution.py:46
  312.3 2.7 fusion.15
  315.0 1.2 copy.49
  316.2 1.2 convolution_convert_fusion.2
  317.4 3.0 copy.50
  320.4 7.9 %all-to-all-start.1 = ((bf16[32,256,256]{2,1,0:T(8,128)(2,1)}), bf16[32,256,256]{2,1,0:T(8,128)(2,1)}, u32[]{:S(2)}, u32[]{:S(2)}) async-start(bf16[32,256,256]{2,1,0:T(8,128)(2,1)} %bitcast.47), calls=%async_computation.1 | async-start | bytes 8388608 | tf_op jit(solution)/shard_map/all_to_all | solution.py:67
  328.3 0.3 all-reduce.6.cloned.1.call-start
  328.6 0.2 dynamic-slice_reduce_fusion
  328.8 50.2 %all-to-all-done.1 = bf16[32,256,256]{2,1,0:T(8,128)(2,1)} async-done(((bf16[32,256,256]{2,1,0:T(8,128)(2,1)}), bf16[32,256,256]{2,1,0:T(8,128)(2,1)}, u32[]{:S(2)}, u32[]{:S(2)}) %all-to-all-start.1) | async-done | bytes 4194336 | tf_op jit(solution)/shard_map/all_to_all | solution.py:67
  379.0 5.0 gather_fusion.3
  384.0 5.0 fusion.16
  389.0 3.3 convolution_bitcast_fusion.1
  392.4 0.0 all-reduce.8.cloned.1.call-start
  392.5 90.7 %all-reduce.6.cloned.1.call-done = f32[16,256,256]{2,1,0:T(8,128)} async-done(((f32[16,256,256]{2,1,0:T(8,128)}), f32[16,256,256]{2,1,0:T(8,128)}) %all-reduce.6.cloned.1.call-update) | async-done | bytes 4194320 | tf_op jit(solution)/shard_map/psum | solution.py:79
  483.1 12.0 %fusion.52 = (bf16[16,256,256]{2,1,0:T(8,128)(2,1)S(1)}, f32[16,256,256]{2,1,0:T(8,128)}) fusion(f32[16,256,256]{2,1,0:T(8,128)} %all-reduce.4.cloned.1.call-done, f32[16]{0:T(128)S(1)} %select_reduce_fusion, f32[16,256]{1,0:T(8,128)S(1)} %copy-done.4, f32[16]{0:T(128)S(1)} %convert_negate_fusion, f32[16,256,256]{2,1,0:T(8,128)} %all-reduce.6.cloned.1.call-done, ...), kind=kOutput, calls=%fused_computation.81 | convolution fusion | flops 1101004800 | bytes 14696640 | tf_op jit(solution)/shard_map/pac,pcd->pad/dot_general | solution.py:84
  495.1 1.2 copy.51
  496.3 1.2 convolution_convert_fusion.1
  497.5 1.0 copy.52
  498.5 58.5 %all_to_all.15 = bf16[32,256,256]{2,1,0:T(8,128)(2,1)} all-to-all(bf16[32,256,256]{2,1,0:T(8,128)(2,1)S(1)} %bitcast.50), channel_id=1, replica_groups=mesh['aux'=4,'pair'=32] {'pair'}, dimensions={0} | all-to-all | bytes 8388608 | tf_op jit(solution)/shard_map/all_to_all | solution.py:67
  557.1 5.0 gather_fusion.4
  562.0 5.0 fusion.19
  567.1 3.3 convolution_bitcast_fusion
  570.4 88.7 %all-reduce.8.cloned.1.call-done = f32[16,256,256]{2,1,0:T(8,128)} async-done(((f32[16,256,256]{2,1,0:T(8,128)}), f32[16,256,256]{2,1,0:T(8,128)}) %all-reduce.8.cloned.1.call-update) | async-done | bytes 4194320 | tf_op jit(solution)/shard_map/psum | solution.py:79
  659.2 12.8 %multiply_reduce_fusion = (f32[16]{0:T(128)S(1)}, bf16[16,256,256]{2,1,0:T(8,128)(2,1)}) fusion(f32[16,256,256]{2,1,0:T(8,128)} %all-reduce.4.cloned.1.call-done, f32[16,256,256]{2,1,0:T(8,128)} %get-tuple-element.13, f32[16,256,256]{2,1,0:T(8,128)} %all-reduce.8.cloned.1.call-done, f32[16]{0:T(128)S(1)} %select_reduce_fusion, f32[16,256]{1,0:T(8,128)S(1)} %copy-done.4, ...), kind=kOutput, calls=%fused_computation.18 | convolution fusion | flops 1092616192 | bytes 14696640 | tf_op jit(solution)/shard_map/pac,pcd->pad/dot_general | solution.py:84
  671.9 0.5 convert_multiply_fusion
  (29 shorter events, 0.2 us)
Async XLA Ops:
  7.2 207.7 %copy-start = (f32[128]{0:T(128)S(1)}, f32[128]{0:T(128)}, u32[]{:S(2)}) copy-start(f32[128]{0:T(128)} %param.16) | copy-start | bytes 1540
  21.2 161.8 %all-to-all-start = ((bf16[32,256,768]{2,1,0:T(8,128)(2,1)}), bf16[32,256,768]{2,1,0:T(8,128)(2,1)}, u32[]{:S(2)}, u32[]{:S(2)}) async-start(bf16[32,256,768]{2,1,0:T(8,128)(2,1)} %bitcast.43), calls=%async_computation | async-start | bytes 25165824 | tf_op jit(solution)/shard_map/all_to_all | solution.py:29
  30.9 281.4 %all-reduce.4.cloned.1.call-start = ((), (), s32[]{:S(2)}) async-start(), calls=%async_computation.3 | async-start | bytes 8388608 | tf_op jit(solution)/shard_map/psum | solution.py:46
  214.9 0.8 copy-start.5
  214.9 1.9 copy-start.6
  214.9 97.3 %copy-start.4 = (f32[16,256]{1,0:T(8,128)S(1)}, f32[16,256]{1,0:T(8,128)}, u32[]{:S(2)}) copy-start(f32[16,256]{1,0:T(8,128)} %param.15) | copy-start | bytes 49156
  320.4 58.6 %all-to-all-start.1 = ((bf16[32,256,256]{2,1,0:T(8,128)(2,1)}), bf16[32,256,256]{2,1,0:T(8,128)(2,1)}, u32[]{:S(2)}, u32[]{:S(2)}) async-start(bf16[32,256,256]{2,1,0:T(8,128)(2,1)} %bitcast.47), calls=%async_computation.1 | async-start | bytes 8388608 | tf_op jit(solution)/shard_map/all_to_all | solution.py:67
  328.3 154.8 %all-reduce.6.cloned.1.call-start = ((), (), s32[]{:S(2)}) async-start(), calls=%async_computation.4 | async-start | bytes 8388608 | tf_op jit(solution)/shard_map/psum | solution.py:79
  384.0 5.0 copy-start.2
  392.4 266.8 %all-reduce.8.cloned.1.call-start = ((), (), s32[]{:S(2)}) async-start(), calls=%async_computation.5 | async-start | bytes 8388608 | tf_op jit(solution)/shard_map/psum | solution.py:79
  562.0 5.0 copy-start.3
  659.2 13.3 %copy-start.1 = (f32[128]{0:T(128)S(1)}, f32[128]{0:T(128)}, u32[]{:S(2)}) copy-start(f32[128]{0:T(128)} %param.16) | copy-start | bytes 1540
Sparse Core Ops, SparseCore 0:
  214.9 97.2 all-reduce.3
  392.5 90.5 all-reduce.5
  570.6 88.5 all-reduce.7
where the time goes:
time: 679 us
  waiting for transfers between devices  477 us (70%)
  matrix products  63.2 us (9%)
  blocking collectives  58.5 us (9%)
  local copies, waits for them, and re-layouts  44.1 us (6%)
  starting transfers between devices  18.1 us (3%)
  between operations  14 us (2%)
    psum x2, waiting for transfers between devices, on_device(): coupled = lax.psum(coupling_terms, 'aux')  179 us
    all_to_all x1, waiting for transfers between devices, on_device(): lax.all_to_all(outgoing, 'pair', split_axis=0, concat_axis=0, tiled=True)  152 us
    psum x1, waiting for transfers between devices, on_device(): coulomb = lax.psum(partial_coulomb, 'aux')  95.4 us
    all_to_all x1, blocking collectives, on_device(): lax.all_to_all(outgoing_amps, 'pair', split_axis=0, concat_axis=0, tiled=...  58.5 us
    all_to_all x1, waiting for transfers between devices, on_device(): lax.all_to_all(outgoing_amps, 'pair', split_axis=0, concat_axis=0, tiled=...  50.2 us
    dot_general x2, matrix products, on_device(): jnp.einsum('pac,pcd->pad', product, local_half, preferred_element_type=jn...  24.8 us
    unnamed x21, local copies, waits for them, and re-layouts  16.3 us
  transfers between devices with their start and end apart: 5, of which 5 were waited for; matrix products, arithmetic and copies ran while one was open for 0% of the time, Pallas kernels for 0%

commit v1 on v0

--- a/solution.py
+++ b/solution.py
@@ -43,7 +43,9 @@
     denominator = pno_energy[:, :, None] + pno_energy[:, None, :] - occupied[:, None, None]
     weights = live.astype(jnp.float32)
     all_refs = partners.reshape(clusters, pair_count, -1)
-    coulomb = lax.psum(partial_coulomb, "aux")
+    coulomb = partial_coulomb
+    for hop in (1, 2):
+        coulomb = coulomb + lax.ppermute(coulomb, "aux", [(dev, dev ^ hop) for dev in range(4)])
     row_refs = lax.dynamic_slice_in_dim(all_refs, aux_row * columns, columns, 2).reshape(
         clusters, pair_count * columns
     )

time: 679 us -> 779 us (1.15)
  waiting for transfers between devices: 477 us -> 549 us
  starting transfers between devices: 18.1 us -> 37.3 us
    ppermute x0 -> x2, waiting for transfers between devices: none -> 166 us  [on_device(): lax.ppermute(coulomb, 'aux', [(dev, dev ^ hop) for dev in range(4)])]
    psum x1 -> x0, waiting for transfers between devices: 95.4 us -> none  [on_device(): coulomb = lax.psum(partial_coulomb, 'aux')]
    all_to_all x1, starting transfers between devices: 7.93 us -> 23.4 us  [on_device(): lax.all_to_all(outgoing_amps, 'pair', split_axis=0, concat_axis=0, tiled=...]
  transfers between devices with their start and end apart: 5 -> 6, of which waited for: 5 -> 6; matrix products, arithmetic and copies ran while one was open for 0% -> 0% of each run, Pallas kernels for 0% -> 0%
where the time goes in v1:
time: 779 us; the launch traced here: 778 us
  waiting for transfers between devices  549 us (70%)
  matrix products  63.5 us (8%)
  blocking collectives  58.5 us (8%)
  local copies, waits for them, and re-layouts  44.1 us (6%)
  starting transfers between devices  37.3 us (5%)
  between operations  14.3 us (2%)
  other arithmetic  11.9 us (2%)
    psum x2, waiting for transfers between devices, on_device(): coupled = lax.psum(coupling_terms, 'aux')  181 us
    ppermute x2, waiting for transfers between devices, on_device(): lax.ppermute(coulomb, 'aux', [(dev, dev ^ hop) for dev in range(4)])  166 us
    all_to_all x1, waiting for transfers between devices, on_device(): lax.all_to_all(outgoing, 'pair', split_axis=0, concat_axis=0, tiled=True)  152 us
    all_to_all x1, blocking collectives, on_device(): lax.all_to_all(outgoing_amps, 'pair', split_axis=0, concat_axis=0, tiled=...  58.5 us
    all_to_all x1, waiting for transfers between devices, on_device(): lax.all_to_all(outgoing_amps, 'pair', split_axis=0, concat_axis=0, tiled=...  50.4 us
    dot_general x2, matrix products, on_device(): jnp.einsum('pac,pcd->pad', product, local_half, preferred_element_type=jn...  25.2 us
    all_to_all x1, starting transfers between devices, on_device(): lax.all_to_all(outgoing_amps, 'pair', split_axis=0, concat_axis=0, tiled=...  23.4 us
    unnamed x21, local copies, waits for them, and re-layouts  16.3 us
  transfers between devices with their start and end apart: 6, of which 6 were waited for; matrix products, arithmetic and copies ran while one was open for 0% of the time, Pallas kernels for 0%

profile of v1, /device:TPU:1, one launch (start us, length us, event | category | flops | bytes accessed | tf_op | source)
XLA Modules:
  0.0 778.5 jit_solution(10935958382452659134)
XLA Ops:
  7.2 0.8 copy.31
  8.0 0.1 eq.30
  8.2 2.6 copy.47
  10.8 0.2 compare_reduce_fusion.1
  11.0 3.7 convolution_convert_fusion
  14.8 6.4 copy.48
  21.2 9.6 %all-to-all-start = ((bf16[32,256,768]{2,1,0:T(8,128)(2,1)}), bf16[32,256,768]{2,1,0:T(8,128)(2,1)}, u32[]{:S(2)}, u32[]{:S(2)}) async-start(bf16[32,256,768]{2,1,0:T(8,128)(2,1)} %bitcast.43), calls=%async_computation | async-start | bytes 25165824 | tf_op jit(solution)/shard_map/all_to_all | solution.py:29
  30.9 0.2 slice_reduce_fusion.1
  31.1 151.9 %all-to-all-done = bf16[32,256,768]{2,1,0:T(8,128)(2,1)} async-done(((bf16[32,256,768]{2,1,0:T(8,128)(2,1)}), bf16[32,256,768]{2,1,0:T(8,128)(2,1)}, u32[]{:S(2)}, u32[]{:S(2)}) %all-to-all-start) | async-done | bytes 12582944 | tf_op jit(solution)/shard_map/all_to_all | solution.py:29
  183.0 8.1 %gather_fusion.2 = bf16[16,256,768]{2,1,0:T(8,128)(2,1)} fusion(bf16[32,256,768]{2,1,0:T(8,128)(2,1)} %all-to-all-done, s32[1024]{0:T(1024)S(1)} %pad_clamp_fusion.2), kind=kCustom, calls=%fused_computation.2.clone | custom fusion | bytes 12582976 | tf_op jit(solution)/shard_map/jit(_take)/gather | solution.py:31
  191.1 6.4 fusion
  197.6 8.1 %gather_fusion.1 = bf16[16,256,768]{2,1,0:T(8,128)(2,1)} fusion(bf16[32,256,768]{2,1,0:T(8,128)(2,1)} %all-to-all-done, s32[1024]{0:T(1024)S(1)} %pad_clamp_fusion.3), kind=kCustom, calls=%fused_computation.clone | custom fusion | bytes 12582976 | tf_op jit(solution)/shard_map/jit(_take)/gather | solution.py:30
  205.7 9.1 %fusion.26 = f32[16,256,256]{2,1,0:T(8,128)} fusion(bf16[16,256,256]{2,1,0:T(8,128)(2,1)S(1)} %fusion, bf16[16,768,256]{2,1,0:T(8,128)(2,1)} %param.13, bf16[16,256,768]{2,1,0:T(8,128)(2,1)} %gather_fusion.1, pred[16]{0:T(512)(128)(4,1)S(1)} %get-tuple-element.20), kind=kOutput, calls=%fused_computation.36 | convolution fusion | flops 2151677952 | bytes 18874384 | tf_op jit(solution)/shard_map/pan,pam->pnm/dot_general | solution.py:39
  214.8 1.2 collective-permute-start
  216.0 82.6 %collective-permute-done = f32[16,256,256]{2,1,0:T(8,128)S(1)} collective-permute-done((f32[16,256,256]{2,1,0:T(8,128)}, f32[16,256,256]{2,1,0:T(8,128)S(1)}, u32[]{:S(2)}, u32[]{:S(2)}) %collective-permute-start) | collective-permute-done | bytes 4194336 | tf_op jit(solution)/shard_map/ppermute | solution.py:48
  298.6 4.9 add.86
  303.5 2.7 collective-permute-start.1
  306.3 0.1 reshape.114
  306.4 0.7 gather_fusion
  307.1 0.1 reshape.113
  307.2 0.1 reshape.71
  307.3 0.1 copy.34
  307.5 0.1 select_reduce_fusion
  307.6 0.7 compare_reduce_fusion
  308.3 83.3 %collective-permute-done.1 = f32[16,256,256]{2,1,0:T(8,128)} collective-permute-done((f32[16,256,256]{2,1,0:T(8,128)}, f32[16,256,256]{2,1,0:T(8,128)}, u32[]{:S(2)}, u32[]{:S(2)}) %collective-permute-start.1) | collective-permute-done | bytes 4194336 | tf_op jit(solution)/shard_map/ppermute | solution.py:48
  391.6 5.3 fusion.15
  397.0 1.2 copy.49
  398.2 1.2 convolution_convert_fusion.2
  399.4 3.0 copy.50
  402.3 23.4 %all-to-all-start.1 = ((bf16[32,256,256]{2,1,0:T(8,128)(2,1)}), bf16[32,256,256]{2,1,0:T(8,128)(2,1)}, u32[]{:S(2)}, u32[]{:S(2)}) async-start(bf16[32,256,256]{2,1,0:T(8,128)(2,1)} %bitcast.47), calls=%async_computation.1 | async-start | bytes 8388608 | tf_op jit(solution)/shard_map/all_to_all | solution.py:69
  425.8 0.2 dynamic-slice_reduce_fusion
  426.0 50.4 %all-to-all-done.1 = bf16[32,256,256]{2,1,0:T(8,128)(2,1)} async-done(((bf16[32,256,256]{2,1,0:T(8,128)(2,1)}), bf16[32,256,256]{2,1,0:T(8,128)(2,1)}, u32[]{:S(2)}, u32[]{:S(2)}) %all-to-all-start.1) | async-done | bytes 4194336 | tf_op jit(solution)/shard_map/all_to_all | solution.py:69
  476.4 5.0 gather_fusion.3
  481.4 5.0 fusion.16
  486.5 3.3 convolution_bitcast_fusion.1
  489.8 0.3 all-reduce.5.cloned.1.call-start
  490.1 91.8 %all-reduce.3.cloned.1.call-done = f32[16,256,256]{2,1,0:T(8,128)} async-done(((f32[16,256,256]{2,1,0:T(8,128)}), f32[16,256,256]{2,1,0:T(8,128)}) %all-reduce.3.cloned.1.call-update) | async-done | bytes 4194320 | tf_op jit(solution)/shard_map/psum | solution.py:81
  581.9 12.4 %fusion.52 = (bf16[16,256,256]{2,1,0:T(8,128)(2,1)S(1)}, f32[16,256,256]{2,1,0:T(8,128)}) fusion(f32[16,256,256]{2,1,0:T(8,128)} %get-tuple-element.9, f32[16]{0:T(128)S(1)} %select_reduce_fusion, f32[16,256]{1,0:T(8,128)S(1)} %copy-done.4, f32[16]{0:T(128)S(1)} %convert_negate_fusion, f32[16,256,256]{2,1,0:T(8,128)} %all-reduce.3.cloned.1.call-done, ...), kind=kOutput, calls=%fused_computation.81 | convolution fusion | flops 1101004800 | bytes 14696640 | tf_op jit(solution)/shard_map/pac,pcd->pad/dot_general | solution.py:86
  594.3 1.2 copy.51
  595.5 1.2 convolution_convert_fusion.1
  596.7 1.0 copy.52
  597.7 58.5 %all_to_all.15 = bf16[32,256,256]{2,1,0:T(8,128)(2,1)} all-to-all(bf16[32,256,256]{2,1,0:T(8,128)(2,1)S(1)} %bitcast.50), channel_id=1, replica_groups=mesh['aux'=4,'pair'=32] {'pair'}, dimensions={0} | all-to-all | bytes 8388608 | tf_op jit(solution)/shard_map/all_to_all | solution.py:69
  656.3 5.0 gather_fusion.4
  661.2 5.0 fusion.19
  666.3 3.3 convolution_bitcast_fusion
  669.6 88.7 %all-reduce.5.cloned.1.call-done = f32[16,256,256]{2,1,0:T(8,128)} async-done(((f32[16,256,256]{2,1,0:T(8,128)}), f32[16,256,256]{2,1,0:T(8,128)}) %all-reduce.5.cloned.1.call-update) | async-done | bytes 4194320 | tf_op jit(solution)/shard_map/psum | solution.py:81
  758.4 12.8 %multiply_reduce_fusion = (f32[16]{0:T(128)S(1)}, bf16[16,256,256]{2,1,0:T(8,128)(2,1)}) fusion(f32[16,256,256]{2,1,0:T(8,128)} %get-tuple-element.9, f32[16,256,256]{2,1,0:T(8,128)} %get-tuple-element.15, f32[16,256,256]{2,1,0:T(8,128)} %all-reduce.5.cloned.1.call-done, f32[16]{0:T(128)S(1)} %select_reduce_fusion, f32[16,256]{1,0:T(8,128)S(1)} %copy-done.4, ...), kind=kOutput, calls=%fused_computation.18 | convolution fusion | flops 1092616192 | bytes 14696640 | tf_op jit(solution)/shard_map/pac,pcd->pad/dot_general | solution.py:86
  771.1 0.5 convert_multiply_fusion
  (31 shorter events, 0.3 us)
Async XLA Ops:
  7.2 299.2 %copy-start = (f32[128]{0:T(128)S(1)}, f32[128]{0:T(128)}, u32[]{:S(2)}) copy-start(f32[128]{0:T(128)} %param.16) | copy-start | bytes 1540
  21.2 161.8 %all-to-all-start = ((bf16[32,256,768]{2,1,0:T(8,128)(2,1)}), bf16[32,256,768]{2,1,0:T(8,128)(2,1)}, u32[]{:S(2)}, u32[]{:S(2)}) async-start(bf16[32,256,768]{2,1,0:T(8,128)(2,1)} %bitcast.43), calls=%async_computation | async-start | bytes 25165824 | tf_op jit(solution)/shard_map/all_to_all | solution.py:29
  214.8 83.8 %collective-permute-start = (f32[16,256,256]{2,1,0:T(8,128)}, f32[16,256,256]{2,1,0:T(8,128)S(1)}, u32[]{:S(2)}, u32[]{:S(2)}) collective-permute-start(f32[16,256,256]{2,1,0:T(8,128)} %fusion.26), channel_id=1, source_target_pairs={{0,32},{32,0},{64,96},{96,64},{1,33},{33,1},{65,97},{97,65},{2,34}... | collective-permute-start | bytes 12582920 | tf_op jit(solution)/shard_map/ppermute | solution.py:48
  303.5 88.1 %collective-permute-start.1 = (f32[16,256,256]{2,1,0:T(8,128)}, f32[16,256,256]{2,1,0:T(8,128)}, u32[]{:S(2)}, u32[]{:S(2)}) collective-permute-start(f32[16,256,256]{2,1,0:T(8,128)} %add.86), channel_id=1, source_target_pairs={{0,64},{32,96},{64,0},{96,32},{1,65},{33,97},{65,1},{97,33},{2,66}... | collective-permute-start | bytes 12582920 | tf_op jit(solution)/shard_map/ppermute | solution.py:48
  306.4 0.8 copy-start.5
  306.4 1.9 copy-start.6
  306.4 85.2 %copy-start.4 = (f32[16,256]{1,0:T(8,128)S(1)}, f32[16,256]{1,0:T(8,128)}, u32[]{:S(2)}) copy-start(f32[16,256]{1,0:T(8,128)} %param.15) | copy-start | bytes 49156
  402.3 74.1 %all-to-all-start.1 = ((bf16[32,256,256]{2,1,0:T(8,128)(2,1)}), bf16[32,256,256]{2,1,0:T(8,128)(2,1)}, u32[]{:S(2)}, u32[]{:S(2)}) async-start(bf16[32,256,256]{2,1,0:T(8,128)(2,1)} %bitcast.47), calls=%async_computation.1 | async-start | bytes 8388608 | tf_op jit(solution)/shard_map/all_to_all | solution.py:69
  425.8 156.1 %all-reduce.3.cloned.1.call-start = ((), (), s32[]{:S(2)}) async-start(), calls=%async_computation.3 | async-start | bytes 8388608 | tf_op jit(solution)/shard_map/psum | solution.py:81
  481.4 5.0 copy-start.2
  489.8 268.6 %all-reduce.5.cloned.1.call-start = ((), (), s32[]{:S(2)}) async-start(), calls=%async_computation.4 | async-start | bytes 8388608 | tf_op jit(solution)/shard_map/psum | solution.py:81
  661.2 5.0 copy-start.3
  758.4 13.3 %copy-start.1 = (f32[128]{0:T(128)S(1)}, f32[128]{0:T(128)}, u32[]{:S(2)}) copy-start(f32[128]{0:T(128)} %param.16) | copy-start | bytes 1540
Sparse Core Ops, SparseCore 0:
  489.9 91.9 all-reduce.2
  669.7 88.5 all-reduce.4
